TPU v7x, 32 devices: a whole 2x2x4 slice. The times are simulated.
32 devices in a mesh: slab: 4 (over y, core), bl: 8 (over z, x).
Axes of the slice: x: 2, y: 2, z: 4, core: 2. Of those that a mesh axis runs over, the one named last changes fastest.
Arguments:
- model_image: float32 [2, 8192, 8192], P(None, 'slab', 'bl'), may hold values from -6 to 6
- vis_coords: float32 [512, 2, 128], P(('slab', 'bl')), may hold values from 0 to 32
- vis_observed: float32 [512, 2, 128], P(('slab', 'bl')), may hold values from -6 to 6
- tile_slot: int32 [512], P(('slab', 'bl')), may hold values from 0 to 2047
- tile_group: int32 [512, 1], P(('slab', 'bl')), may hold values from 0 to 7; in each aligned block of 16 rows (0 to 15, 16 to 31, ...) at most 8 rows name the same one
- w_plane: int32 [512], P(('slab', 'bl')), may hold values from 0 to 7
- vis_count: int32 [512], P(('slab', 'bl')), may hold values from 16 to 128, as said below
Outputs:
- residual_image: float32 [2, 8192, 8192], P(None, 'slab', 'bl')
- residual_vis: float32 [512, 2, 128], P(('slab', 'bl'))
Inputs may be any that keep to these rules, and one draw needn't show every extreme that they name: `tile_group`: among the 16 subgrids of one device, at most 8 name the same group. `vis_count`: some subgrid holds exactly 128 visibilities.
All inputs are finite; a program needn't handle non-finite values.
Results may differ from a plain program's by a relative error of at most 0.0003.
Values sent between devices are 32-bit elements; how exact they have to be, the bound alone decides.
No kernel may reach another device: no remote copies, remote signals or barrier semaphores. Data moves between devices by JAX's collectives and lax.ppermute only.
A program may use at most 192 MiB of HBM per device.

v0:
```python
import math

import jax
import jax.numpy as jnp
from jax import lax
from jax.sharding import PartitionSpec as P

N = 8192
SUB = 32
FA = 128


w_step = 0.1


def complex_einsum(form, left, right):
    product = lambda first, second: jnp.einsum(form, first, second, precision=lax.Precision.HIGHEST)
    return (
        product(left[0], right[0]) - product(left[1], right[1]),
        product(left[0], right[1]) + product(left[1], right[0]),
    )


def complex_mul(left, right):
    return (left[0] * right[0] - left[1] * right[1], left[0] * right[1] + left[1] * right[0])


def subgrid_pass(tile_real, tile_imag, coords, observed, planes, counts):
    width = tile_real.shape[-1]
    half = width // 2
    slots = coords.shape[-1]
    index = jnp.arange(width, dtype=jnp.int32)
    offsets = (index - half).astype(jnp.float32)
    turns = index[:, None] * (index[None, :] - half) % width
    angle = 2.0 * math.pi / width * turns.astype(jnp.float32)
    forward_d = (jnp.cos(angle), jnp.sin(angle))
    backward_d = (forward_d[0], -forward_d[1])
    scale_sub = 1.0 / (width * width)
    halfway = complex_einsum("il,kij->klj", forward_d, (tile_real, tile_imag))
    image_sub = complex_einsum("klj,jm->klm", halfway, forward_d)
    image_sub = (image_sub[0] * scale_sub, image_sub[1] * scale_sub)
    radius = (offsets[:, None] ** 2 + offsets[None, :] ** 2) / (half * half)
    phase = -w_step * planes.astype(jnp.float32)[:, None, None] * radius[None]
    screen = (jnp.cos(phase), jnp.sin(phase))
    weighted = complex_mul(screen, image_sub)
    along_a = -2.0 * math.pi / width * coords[:, 0, :][:, None, :] * offsets[None, :, None]
    along_b = -2.0 * math.pi / width * coords[:, 1, :][:, None, :] * offsets[None, :, None]
    phase_a = (jnp.cos(along_a), jnp.sin(along_a))
    phase_b = (jnp.cos(along_b), jnp.sin(along_b))
    partial_rows = complex_einsum("klm,kmj->klj", weighted, phase_b)
    terms = complex_mul(phase_a, partial_rows)
    predicted = (jnp.sum(terms[0], axis=1), jnp.sum(terms[1], axis=1))
    live = (jnp.arange(slots, dtype=jnp.int32)[None, :] < counts[:, None]).astype(jnp.float32)
    resid_real = (observed[:, 0, :] - predicted[0]) * live
    resid_imag = (observed[:, 1, :] - predicted[1]) * live
    spread = complex_mul(
        (phase_a[0], -phase_a[1]), (resid_real[:, None, :], resid_imag[:, None, :])
    )
    collected = complex_einsum("klj,kmj->klm", spread, (phase_b[0], -phase_b[1]))
    unscreened = complex_mul((screen[0], -screen[1]), collected)
    middle = complex_einsum("il,klm->kim", backward_d, unscreened)
    tile_out = complex_einsum("kim,jm->kij", middle, backward_d)
    return (
        jnp.stack([resid_real, resid_imag], axis=1),
        jnp.stack([tile_out[0] * scale_sub, tile_out[1] * scale_sub], axis=1),
    )


def run_blocks(tile_stack, coords, observed, planes, counts):
    total = tile_stack.shape[0]
    slots = coords.shape[-1]
    width = tile_stack.shape[-1]
    block_size = math.gcd(total, 64)
    block_count = total // block_size

    def one_block(pieces):
        block_tiles, block_coords, block_obs, block_planes, block_counts = pieces
        return subgrid_pass(
            block_tiles[:, 0],
            block_tiles[:, 1],
            block_coords,
            block_obs,
            block_planes,
            block_counts,
        )

    resid_vis, contrib = lax.map(
        one_block,
        (
            tile_stack.reshape(block_count, block_size, 2, width, width),
            coords.reshape(block_count, block_size, 2, slots),
            observed.reshape(block_count, block_size, 2, slots),
            planes.reshape(block_count, block_size),
            counts.reshape(block_count, block_size),
        ),
    )
    return (resid_vis.reshape(total, 2, slots), contrib.reshape(total, 2 * width * width))


def dft_table(rows_count, cols_count, modulus, turn_sign):
    product = (
        lax.broadcasted_iota(jnp.int32, (rows_count, cols_count), 0)
        * lax.broadcasted_iota(jnp.int32, (rows_count, cols_count), 1)
        % modulus
    )
    angle = 2.0 * math.pi / modulus * product.astype(jnp.float32)
    return (jnp.cos(angle), turn_sign * jnp.sin(angle))


def dft_last(real_part, imag_part, turn_sign):
    length = real_part.shape[-1]
    inner = FA
    outer = length // inner
    leading = real_part.shape[:-1]
    outer_table = dft_table(outer, outer, outer, turn_sign)
    twiddle = dft_table(outer, inner, length, turn_sign)
    inner_table = dft_table(inner, inner, inner, turn_sign)
    shaped = (
        real_part.reshape(leading + (outer, inner)),
        imag_part.reshape(leading + (outer, inner)),
    )
    first_pass = complex_einsum("...ca,vc->...va", shaped, outer_table)
    first_pass = complex_mul(first_pass, twiddle)
    second_pass = complex_einsum("...va,wa->...wv", first_pass, inner_table)
    return (
        second_pass[0].reshape(leading + (length,)),
        second_pass[1].reshape(leading + (length,)),
    )


def to_columns(block):
    groups = lax.axis_size("bl")
    bands = lax.axis_size("slab")
    depth = block.shape[1]
    peers = block.shape[2] // depth
    packed = (
        block.reshape(2, depth, peers, depth)
        .transpose(0, 2, 1, 3)
        .reshape(2, 1, peers, depth * depth)
    )
    moved = lax.all_to_all(
        lax.all_to_all(packed, "slab", split_axis=2, concat_axis=1, tiled=True),
        "bl",
        split_axis=2,
        concat_axis=1,
        tiled=True,
    )
    shaped = moved.reshape(2, groups, bands, depth, depth)
    return shaped.transpose(0, 4, 2, 1, 3).reshape(2, depth, groups * bands * depth)


def per_device(model_image, vis_coords, vis_observed, tile_slot, tile_group, w_plane, vis_count):
    groups = lax.axis_size("bl")
    spread_rows = lax.all_to_all(model_image, "bl", split_axis=1, concat_axis=2, tiled=True)
    col_real, col_imag = dft_last(spread_rows[0], spread_rows[1], -1.0)
    turned = to_columns(jnp.stack([col_real, col_imag]))
    grid_real, grid_imag = dft_last(turned[0], turned[1], -1.0)
    grid_block = jnp.stack([grid_real, grid_imag]) / N
    depth = grid_block.shape[1]
    owned_cols = depth // SUB
    tile_rows = N // SUB
    table = grid_block.reshape(2, owned_cols, SUB, tile_rows, SUB).transpose(1, 3, 0, 4, 2)
    table = table.reshape(owned_cols * tile_rows, 2 * SUB * SUB)
    table_rows = table.shape[0]
    sub_count = tile_slot.shape[0]
    capacity = max(2, 4 * sub_count // groups)
    buckets = groups * capacity
    owner = tile_group[:, 0]
    onehot = (owner[:, None] == jnp.arange(groups, dtype=jnp.int32)[None, :]).astype(jnp.int32)
    rank = jnp.sum(jnp.cumsum(onehot, axis=0) * onehot, axis=1) - 1
    bucket = owner * capacity + rank
    requests = jnp.zeros((buckets,), jnp.int32).at[bucket].set(tile_slot)
    asked = lax.all_to_all(requests, "bl", split_axis=0, concat_axis=0, tiled=True)
    fetched = lax.all_to_all(table[asked], "bl", split_axis=0, concat_axis=0, tiled=True)
    mine = fetched[bucket].reshape(sub_count, 2, SUB, SUB)
    residual_vis, contrib = run_blocks(mine, vis_coords, vis_observed, w_plane, vis_count)
    outgoing = jnp.zeros((buckets, 2 * SUB * SUB), jnp.float32).at[bucket].set(contrib)
    arriving = lax.all_to_all(outgoing, "bl", split_axis=0, concat_axis=0, tiled=True)
    summed = jax.ops.segment_sum(arriving, asked, num_segments=table_rows)
    resid_block = (
        summed.reshape(owned_cols, tile_rows, 2, SUB, SUB)
        .transpose(2, 0, 4, 1, 3)
        .reshape(2, depth, N)
    )
    inv_real, inv_imag = dft_last(resid_block[0], resid_block[1], 1.0)
    turned_back = to_columns(jnp.stack([inv_real, inv_imag]))
    out_real, out_imag = dft_last(turned_back[0], turned_back[1], 1.0)
    residual_image = lax.all_to_all(
        jnp.stack([out_real, out_imag]) / N, "bl", split_axis=2, concat_axis=1, tiled=True
    )
    return (residual_image, residual_vis)


def solution(mesh):
    placed = (
        P(None, "slab", "bl"),
        P(("slab", "bl"), None, None),
        P(("slab", "bl"), None, None),
        P(("slab", "bl")),
        P(("slab", "bl"), None),
        P(("slab", "bl")),
        P(("slab", "bl")),
    )
    return jax.shard_map(
        per_device,
        mesh=mesh,
        in_specs=placed,
        out_specs=(P(None, "slab", "bl"), P(("slab", "bl"), None, None)),
        check_vma=False,
    )
```

profile of v0, /device:TPU:0, one launch (start us, length us, event | category | flops | bytes accessed | tf_op | source)
XLA Modules:
  0.0 3178.1 jit_solution(16493130110387688211)
XLA Ops:
  0.6 28.6 copy.141
  36.7 362.8 %all-to-all-done.1 = f32[2,2048,1024]{2,0,1:T(2,128)} async-done(((f32[2,2048,1024]{2,0,1:T(2,128)}), f32[2,2048,1024]{2,0,1:T(2,128)}, u32[]{:S(2)}, u32[]{:S(2)}) %all-to-all-start.1) | async-done | bytes 16777248 | tf_op jit(solution)/shard_map/all_to_all | solution.py:154
  399.5 15.2 copy.283
  430.8 12.8 fusion.179
  462.9 11.8 fusion.177
  474.7 19.8 subtract_bitcast_fusion.7
  494.5 18.6 fusion.29
  513.2 12.7 fusion.27
  525.9 19.3 subtract_bitcast_fusion.6
  545.2 11.5 copy.145
  556.8 17.9 add_bitcast_fusion.6
  589.3 17.5 copy.216
  606.8 27.2 reshape.307
  642.9 181.3 %all-to-all-done.2 = f32[2,1,32,65536]{3,0,1,2:T(2,128)} async-done(((f32[2,1,32,65536]{3,0,1,2:T(2,128)}), f32[2,1,32,65536]{3,0,1,2:T(2,128)}, u32[]{:S(2)}, u32[]{:S(2)}) %all-to-all-start.2) | async-done | bytes 16777248 | tf_op jit(solution)/shard_map/all_to_all | solution.py:142
  827.7 20.9 copy.151
  856.1 361.0 %all-to-all-done.3 = f32[2,4,8,65536]{3,1,0,2:T(4,128)} async-done(((f32[2,4,8,65536]{3,1,0,2:T(4,128)}), f32[2,4,8,65536]{3,1,0,2:T(4,128)}, u32[]{:S(2)}, u32[]{:S(2)}) %all-to-all-start.3) | async-done | bytes 16777248 | tf_op jit(solution)/shard_map/all_to_all | solution.py:141
  1217.1 20.5 reshape.308
  1259.5 12.8 fusion.175
  1290.8 12.1 fusion.173
  1302.9 19.4 subtract_bitcast_fusion.5
  1322.4 16.7 fusion.21
  1339.1 17.1 fusion.19
  1356.2 17.8 subtract_bitcast_fusion.4
  1385.5 20.5 stack.47
  1406.1 22.9 copy.161
  1428.9 18.3 add_bitcast_fusion.4
  1455.7 20.5 stack.48
  1476.3 22.4 copy.162
  1505.5 17.6 copy.163
  1534.4 18.0 copy.164
  1563.9 14.6 all-to-all-done.4
  1620.0 13.3 all-to-all-done.5
  1641.9 18.0 copy.180
  1677.4 19.6 copy.182
  1697.0 23.0 reshape_squeeze.29
  1719.9 12.9 fusion.171
  1742.7 19.6 copy.181
  1762.3 23.0 reshape_squeeze.28
  1785.3 11.9 fusion.169
  1797.2 19.8 subtract_bitcast_fusion.3
  1817.1 18.6 fusion.13
  1835.7 12.7 fusion.11
  1848.4 19.3 subtract_bitcast_fusion.2
  1867.7 11.5 copy.185
  1879.3 17.9 add_bitcast_fusion.2
  1911.8 17.5 copy.220
  1929.3 27.2 reshape.309
  1956.5 187.7 %all_to_all.120 = f32[2,1,32,65536]{3,0,1,2:T(2,128)S(1)} all-to-all(f32[2,1,32,65536]{3,0,1,2:T(2,128)} %reshape.309), channel_id=1, replica_groups=mesh['slab'=4,'bl'=8] {'slab'}, dimensions={2} | all-to-all | bytes 33554432 | tf_op jit(solution)/shard_map/all_to_all | solution.py:142
  2144.2 19.1 copy.191
  2163.3 366.7 %all_to_all.121 = f32[2,4,8,65536]{3,1,0,2:T(4,128)} all-to-all(f32[2,4,8,65536]{3,1,0,2:T(4,128)S(1)} %copy.191), channel_id=1, replica_groups=mesh['slab'=4,'bl'=8] {'bl'}, dimensions={2} | all-to-all | bytes 33554432 | tf_op jit(solution)/shard_map/all_to_all | solution.py:141
  2530.1 20.5 reshape.310
  2572.5 12.8 fusion.167
  2603.8 12.2 fusion.165
  2616.0 19.5 subtract_bitcast_fusion.1
  2635.5 18.6 fusion.5
  2654.1 12.9 fusion.3
  2667.1 19.3 subtract_bitcast_fusion
  2686.4 11.5 copy.197
  2697.9 17.8 add_bitcast_fusion
  2715.7 11.5 copy.200
  2733.7 46.1 %copy.201 = f32[2,256,8192]{1,0,2:T(2,128)} copy(f32[2,256,8192]{1,2,0:T(8,128)S(1)} %maximum_multiply_fusion.1) | data formatting | bytes 33554432 | tf_op jit(solution)/shard_map/div | solution.py:189
  2786.3 361.3 %all-to-all-done.8 = f32[2,256,8192]{1,0,2:T(2,128)} async-done(((f32[2,256,8192]{1,0,2:T(2,128)}), f32[2,256,8192]{1,0,2:T(2,128)}, u32[]{:S(2)}, u32[]{:S(2)}) %all-to-all-start.8) | async-done | bytes 16777248 | tf_op jit(solution)/shard_map/all_to_all | solution.py:188
  3147.7 12.7 copy.202
  3160.4 17.3 copy.203
  (161 shorter events, 312.5 us)
Async XLA Ops:
  29.2 370.3 %all-to-all-start.1 = ((f32[2,2048,1024]{2,0,1:T(2,128)}), f32[2,2048,1024]{2,0,1:T(2,128)}, u32[]{:S(2)}, u32[]{:S(2)}) async-start(f32[2,2048,1024]{2,0,1:T(2,128)} %copy.141), calls=%async_computation.1 | async-start | bytes 33554432 | tf_op jit(solution)/shard_map/all_to_all | solution.py:154
  36.7 1266.3 %copy-start.10 = (f32[64,128]{1,0:T(8,128)}, f32[64,128]{1,0:T(8,128)S(1)}, u32[]{:S(2)}) copy-start(f32[64,128]{1,0:T(8,128)S(1)} %get-tuple-element.49) | copy-start | bytes 98308
  430.8 12.9 copy-start.1
  494.5 18.6 copy-start.6
  494.5 31.4 slice-start.4
  513.2 12.7 slice-start.5
  574.7 8.4 copy-start.8
  634.0 7.1 copy-start.21
  634.0 190.2 %all-to-all-start.2 = ((f32[2,1,32,65536]{3,0,1,2:T(2,128)}), f32[2,1,32,65536]{3,0,1,2:T(2,128)}, u32[]{:S(2)}, u32[]{:S(2)}) async-start(f32[2,1,32,65536]{3,0,1,2:T(2,128)} %reshape.307), calls=%async_computation.2 | async-start | bytes 33554432 | tf_op jit(solution)/shard_map/all_to_all | solution.py:142
  641.4 182.7 %copy-start.23 = (s32[16]{0:T(128)}, s32[16]{0:T(128)S(1)}, u32[]{:S(2)}) copy-start(s32[16]{0:T(128)S(1)} %fusion.304) | copy-start | bytes 196
  824.2 24.4 all-to-all-start
  848.6 6.9 copy-start.13
  848.6 368.6 %all-to-all-start.3 = ((f32[2,4,8,65536]{3,1,0,2:T(4,128)}), f32[2,4,8,65536]{3,1,0,2:T(4,128)}, u32[]{:S(2)}, u32[]{:S(2)}) async-start(f32[2,4,8,65536]{3,1,0,2:T(4,128)} %copy.151), calls=%async_computation.3 | async-start | bytes 33554432 | tf_op jit(solution)/shard_map/all_to_all | solution.py:141
  1259.5 12.8 copy-start.2
  1322.4 16.7 copy-start.5
  1322.4 33.8 %slice-start = ((s8[8388608]{0:T(1024)(128)(4,1)}), s8[4194304]{0:T(1024)(128)(4,1)S(1)}, s32[]{:S(2)}) async-start(s8[8388608]{0:T(1024)(128)(4,1)} %bitcast.293), calls=%async_computation.9 | async-start | bytes 8388608
  1339.1 17.1 slice-start.1
  1534.3 29.4 copy-start.24
  1534.3 29.4 copy-start.25
  1534.3 29.5 copy-start.20
  1534.4 44.9 %copy-start.12 = (s32[32]{0:T(128)S(1)}, s32[32]{0:T(128)}, u32[]{:S(2)}) copy-start(s32[32]{0:T(128)} %iota_add_fusion) | copy-start | bytes 388
  1552.4 42.0 %copy-start.19 = (f32[16,2,128]{2,1,0:T(2,128)S(1)}, f32[16,2,128]{2,1,0:T(2,128)}, u32[]{:S(2)}) copy-start(f32[16,2,128]{2,1,0:T(2,128)} %param.9) | copy-start | bytes 49156
  1552.4 42.0 %copy-start.22 = (s32[16]{0:T(128)S(1)}, s32[16]{0:T(128)}, u32[]{:S(2)}) copy-start(s32[16]{0:T(128)} %param.13) | copy-start | bytes 196
  1560.1 18.4 all-to-all-start.4
  1586.3 33.0 %copy-start.14 = (s32[8,8,1]{1,2,0:T(1,128)S(1)}, s32[8,8,1]{1,2,0:T(1,128)}, u32[]{:S(2)}) copy-start(s32[8,8,1]{1,2,0:T(1,128)} %copy-done.13) | copy-start | bytes 772
  1594.5 18.8 copy-start.17
  1594.5 47.4 %copy-start.15 = (f32[16,1,128]{2,1,0:T(1,128)}, f32[16,1,128]{2,1,0:T(1,128)S(1)}, u32[]{:S(2)}) copy-start(f32[16,1,128]{2,1,0:T(1,128)S(1)} %get-tuple-element.44) | copy-start | bytes 24580
  1615.0 18.3 all-to-all-start.5
  1719.9 12.9 copy-start
  1785.3 11.9 copy-start.11
  1817.0 18.6 copy-start.7
  1817.0 31.3 slice-start.6
  1835.7 12.7 slice-start.7
  1897.2 8.4 copy-start.9
  2572.5 12.8 copy-start.3
  2635.5 18.6 copy-start.4
  2635.5 31.6 slice-start.2
  2654.1 13.0 slice-start.3
  2779.8 5.9 copy-start.16
  2779.8 5.9 copy-start.18
  2779.8 367.9 %all-to-all-start.8 = ((f32[2,256,8192]{1,0,2:T(2,128)}), f32[2,256,8192]{1,0,2:T(2,128)}, u32[]{:S(2)}, u32[]{:S(2)}) async-start(f32[2,256,8192]{1,0,2:T(2,128)} %copy.201), calls=%async_computation.8 | async-start | bytes 33554432 | tf_op jit(solution)/shard_map/all_to_all | solution.py:188
where the time goes:
time: 3190 us; the launch traced here: 3180 us
  waiting for transfers between devices  1290 us (40%)
  local copies, waits for them, and re-layouts  726 us (23%)
  blocking collectives  554 us (17%)
  matrix products  527 us (17%)
  other arithmetic  37.6 us (1%)
  starting transfers between devices  37.3 us (1%)
    dot_general x56, matrix products, complex_einsum(): jnp.einsum(form, first, second, precision=lax.Precision.HIGHEST)  527 us
    all_to_all x1, blocking collectives, to_columns(): lax.all_to_all(lax.all_to_all(packed, 'slab', split_axis=2, concat_axis=1...  367 us
    all_to_all x1, waiting for transfers between devices, per_device(): lax.all_to_all(model_image, 'bl', split_axis=1, concat_axis=2, tiled=True)  363 us
    all_to_all x1, waiting for transfers between devices, per_device(): lax.all_to_all(jnp.stack([out_real, out_imag]) / N, 'bl', split_axis=2, c...  361 us
    all_to_all x1, waiting for transfers between devices, to_columns(): lax.all_to_all(lax.all_to_all(packed, 'slab', split_axis=2, concat_axis=1...  361 us
    all_to_all x1, blocking collectives, to_columns(): lax.all_to_all(packed, 'slab', split_axis=2, concat_axis=1, tiled=True)  188 us
    all_to_all x1, waiting for transfers between devices, to_columns(): lax.all_to_all(packed, 'slab', split_axis=2, concat_axis=1, tiled=True)  181 us
    reshape x4, local copies, waits for them, and re-layouts, to_columns(): packed = block.reshape(2, depth, peers, depth).transpose(0, 2, 1, 3).resh...  89.4 us
  transfers between devices with their start and end apart: 7, of which 6 were waited for; matrix products, arithmetic and copies ran while one was open for 1% of the time, Pallas kernels for 0%

commit v1 on v0

v1 whole, which is shorter than its diff:
```python
import math

import jax
import jax.numpy as jnp
from jax import lax
from jax.sharding import PartitionSpec as P

SUB = 32


w_step = 0.1


def complex_einsum(form, left, right):
    product = lambda first, second: jnp.einsum(form, first, second, precision=lax.Precision.HIGHEST)
    return (
        product(left[0], right[0]) - product(left[1], right[1]),
        product(left[0], right[1]) + product(left[1], right[0]),
    )


def complex_mul(left, right):
    return (left[0] * right[0] - left[1] * right[1], left[0] * right[1] + left[1] * right[0])


def subgrid_pass(tile_real, tile_imag, coords, observed, planes, counts):
    width = tile_real.shape[-1]
    half = width // 2
    slots = coords.shape[-1]
    index = jnp.arange(width, dtype=jnp.int32)
    offsets = (index - half).astype(jnp.float32)
    turns = index[:, None] * (index[None, :] - half) % width
    angle = 2.0 * math.pi / width * turns.astype(jnp.float32)
    forward_d = (jnp.cos(angle), jnp.sin(angle))
    backward_d = (forward_d[0], -forward_d[1])
    scale_sub = 1.0 / (width * width)
    halfway = complex_einsum("il,kij->klj", forward_d, (tile_real, tile_imag))
    image_sub = complex_einsum("klj,jm->klm", halfway, forward_d)
    image_sub = (image_sub[0] * scale_sub, image_sub[1] * scale_sub)
    radius = (offsets[:, None] ** 2 + offsets[None, :] ** 2) / (half * half)
    phase = -w_step * planes.astype(jnp.float32)[:, None, None] * radius[None]
    screen = (jnp.cos(phase), jnp.sin(phase))
    weighted = complex_mul(screen, image_sub)
    along_a = -2.0 * math.pi / width * coords[:, 0, :][:, None, :] * offsets[None, :, None]
    along_b = -2.0 * math.pi / width * coords[:, 1, :][:, None, :] * offsets[None, :, None]
    phase_a = (jnp.cos(along_a), jnp.sin(along_a))
    phase_b = (jnp.cos(along_b), jnp.sin(along_b))
    partial_rows = complex_einsum("klm,kmj->klj", weighted, phase_b)
    terms = complex_mul(phase_a, partial_rows)
    predicted = (jnp.sum(terms[0], axis=1), jnp.sum(terms[1], axis=1))
    live = (jnp.arange(slots, dtype=jnp.int32)[None, :] < counts[:, None]).astype(jnp.float32)
    resid_real = (observed[:, 0, :] - predicted[0]) * live
    resid_imag = (observed[:, 1, :] - predicted[1]) * live
    spread = complex_mul(
        (phase_a[0], -phase_a[1]), (resid_real[:, None, :], resid_imag[:, None, :])
    )
    collected = complex_einsum("klj,kmj->klm", spread, (phase_b[0], -phase_b[1]))
    unscreened = complex_mul((screen[0], -screen[1]), collected)
    middle = complex_einsum("il,klm->kim", backward_d, unscreened)
    tile_out = complex_einsum("kim,jm->kij", middle, backward_d)
    return (
        jnp.stack([resid_real, resid_imag], axis=1),
        jnp.stack([tile_out[0] * scale_sub, tile_out[1] * scale_sub], axis=1),
    )


def table(product, modulus, sign):
    angle = 2.0 * math.pi / modulus * (product % modulus).astype(jnp.float32)
    return jnp.cos(angle), sign * jnp.sin(angle)


def real_form(pair):
    return jnp.stack([jnp.stack([pair[0], -pair[1]], axis=1), jnp.stack([pair[1], pair[0]], axis=1)], axis=0)


def product_high(form, left, right):
    return jnp.einsum(form, left, right, precision=lax.Precision.HIGH)


def twist(pair, values):
    return jnp.stack(complex_mul(pair, (values[0], values[1])))


def per_device(model_image, vis_coords, vis_observed, tile_slot, tile_group, w_plane, vis_count):
    groups = lax.axis_size("bl")
    bands = lax.axis_size("slab")
    both = ("slab", "bl")
    width_in = model_image.shape[2]
    extent = model_image.shape[1] * bands
    tile_rows = extent // SUB
    owned_cols = tile_rows // (groups * bands)
    sub_count = tile_slot.shape[0]

    tile_u = tile_slot % tile_rows
    tile_v = (lax.axis_index("slab") * groups + tile_group[:, 0]) * owned_cols + tile_slot // tile_rows
    ids = lax.all_gather(tile_u * tile_rows + tile_v, both, axis=0, tiled=True)
    all_u = ids // tile_rows
    all_v = ids % tile_rows

    image = lax.all_to_all(model_image, "slab", split_axis=2, concat_axis=1, tiled=True)
    cols = image.shape[2]
    col = lax.axis_index("bl") * width_in + lax.axis_index("slab") * cols + jnp.arange(cols, dtype=jnp.int32)
    short = jnp.arange(SUB, dtype=jnp.int32)
    long = jnp.arange(tile_rows, dtype=jnp.int32)

    coarse = table(short[:, None] * short[None, :], SUB, -1.0)
    fine = table(short[:, None] * long[None, :], extent, -1.0)
    pick_u = table(all_u[:, None] * long[None, :], tile_rows, -1.0)
    shift_v = table(all_v[:, None] * col[None, :], tile_rows, -1.0)
    inside_v = table(short[:, None] * col[None, :], extent, -1.0)
    conj = lambda pair: (pair[0], -pair[1])
    lift_fine = lambda pair: (pair[0][:, :, None], pair[1][:, :, None])
    lift_v = lambda pair: (pair[0][:, None, :], pair[1][:, None, :])

    stage = product_high("aibq,bqpc->aipc", real_form(coarse), image.reshape(2, SUB, tile_rows, cols))
    stage = twist(lift_fine(fine), stage)
    strips = product_high("agbp,bipc->agic", real_form(pick_u), stage)
    strips = twist(lift_v(shift_v), strips)
    partial = product_high("ajbc,bgic->gaij", real_form(inside_v), strips) / extent
    mine = lax.psum_scatter(partial.reshape(-1, 2 * SUB * SUB), both, scatter_dimension=0, tiled=True)
    mine = mine.reshape(sub_count, 2, SUB, SUB)
    residual_vis, contrib = subgrid_pass(mine[:, 0], mine[:, 1], vis_coords, vis_observed, w_plane, vis_count)
    every = lax.all_gather(contrib.reshape(sub_count, 2 * SUB * SUB), both, axis=0, tiled=True)
    every = every.reshape(-1, 2, SUB, SUB)
    spread = product_high("ajbc,gaij->bgic", real_form(inside_v), every)
    spread = twist(lift_v(conj(shift_v)), spread)
    back = product_high("agbp,agic->bipc", real_form(pick_u), spread)
    back = twist(lift_fine(conj(fine)), back) / extent
    rows = product_high("aibq,aipc->bqpc", real_form(coarse), back)
    residual_image = lax.all_to_all(
        rows.reshape(2, extent, cols), "slab", split_axis=1, concat_axis=2, tiled=True
    )
    return (residual_image, residual_vis)


def solution(mesh):
    placed = (
        P(None, "slab", "bl"),
        P(("slab", "bl"), None, None),
        P(("slab", "bl"), None, None),
        P(("slab", "bl")),
        P(("slab", "bl"), None),
        P(("slab", "bl")),
        P(("slab", "bl")),
    )
    return jax.shard_map(
        per_device,
        mesh=mesh,
        in_specs=placed,
        out_specs=(P(None, "slab", "bl"), P(("slab", "bl"), None, None)),
        check_vma=False,
    )
```

time: 3190 us -> 1130 us (0.35)
  waiting for transfers between devices: 1290 us -> 384 us
  local copies, waits for them, and re-layouts: 726 us -> 213 us
  blocking collectives: 554 us -> 219 us
  matrix products: 527 us -> 194 us
  other arithmetic: 37.6 us -> 79.1 us
    all_to_all x7 -> x2, waiting for transfers between devices: 1290 us -> 182 us  [the longest x1 182 us: per_device(): lax.all_to_all(rows.reshape(2, extent, cols), 'slab', split_axis=1, conca...]
    all_to_all x2 -> x0, blocking collectives: 554 us -> none  [the longest x1 367 us: to_columns(): lax.all_to_all(lax.all_to_all(packed, 'slab', split_axis=2, concat_axis=1...]
    dot_general x56 -> x24, matrix products: 527 us -> 36.2 us  [complex_einsum(): jnp.einsum(form, first, second, precision=lax.Precision.HIGHEST)]
    unnamed x0 -> x1, blocking collectives: none -> 219 us
    another operation x12 -> x0, local copies, waits for them, and re-layouts: 186 us -> none  [the longest x4 86.3 us: per_device(): grid_block = jnp.stack([grid_real, grid_imag]) / N]
    dot_general x0 -> x6, matrix products: none -> 158 us  [product_high(): return jnp.einsum(form, left, right, precision=lax.Precision.HIGH)]
    unnamed x0 -> x3, waiting for transfers between devices: none -> 144 us
    reshape x10 -> x2, local copies, waits for them, and re-layouts: 162 us -> 47 us  [the longest x1 46.1 us: per_device(): rows.reshape(2, extent, cols)]
  transfers between devices with their start and end apart: 7 -> 4, of which waited for: 6 -> 3; matrix products, arithmetic and copies ran while one was open for 1% -> 1% of each run, Pallas kernels for 0% -> 0%
where the time goes in v1:
time: 1130 us; the launch traced here: 1120 us
  waiting for transfers between devices  384 us (34%)
  blocking collectives  219 us (19%)
  local copies, waits for them, and re-layouts  213 us (19%)
  matrix products  194 us (17%)
  other arithmetic  79.1 us (7%)
  between operations  14.9 us (1%)
  starting transfers between devices  14.4 us (1%)
    unnamed x1, blocking collectives  219 us
    all_to_all x1, waiting for transfers between devices, per_device(): lax.all_to_all(rows.reshape(2, extent, cols), 'slab', split_axis=1, conca...  182 us
    dot_general x6, matrix products, product_high(): return jnp.einsum(form, left, right, precision=lax.Precision.HIGH)  158 us
    unnamed x3, waiting for transfers between devices  144 us
    sub x4, other arithmetic, complex_mul(): left[0] * right[0] - left[1] * right[1]  62.7 us
    all_gather x1, waiting for transfers between devices, per_device(): lax.all_gather(contrib.reshape(sub_count, 2 * SUB * SUB), both, axis=0, t...  57.8 us
    unnamed x37, local copies, waits for them, and re-layouts  53.7 us
    reshape x1, local copies, waits for them, and re-layouts, per_device(): rows.reshape(2, extent, cols)  46.1 us
  transfers between devices with their start and end apart: 4, of which 3 were waited for; matrix products, arithmetic and copies ran while one was open for 1% of the time, Pallas kernels for 0%

profile of v1, /device:TPU:0, one launch (start us, length us, event | category | flops | bytes accessed | tf_op | source)
XLA Modules:
  0.0 1117.9 jit_solution(155449338450149249)
XLA Ops:
  7.2 25.3 %copy.94 = f32[2,2048,1024]{1,0,2:T(2,128)} copy(f32[2,2048,1024]{2,1,0:T(8,128)} %param.7) | data formatting | bytes 33554432 | tf_op args[0]
  32.5 7.1 all-to-all-start
  39.8 218.7 %all-reduce = s32[512]{0:T(512)S(1)} all-reduce(s32[512]{0:T(512)S(1)} %fusion.206), channel_id=1, replica_groups=mesh['slab'=4,'bl'=8] {'slab','bl'}, use_global_device_ids=true, to_apply=%add | all-reduce | flops 512 | bytes 4096
  258.8 1.2 sine_multiply_fusion.2
  260.1 2.1 fusion.95
  262.4 3.2 fusion.96
  265.5 17.7 %copy.95 = f32[2,2048,1024]{1,2,0:T(8,128)} copy(f32[2,2048,1024]{1,0,2:T(2,128)} %all-to-all-done) | data formatting | bytes 33554432 | tf_op jit(solution)/shard_map/all_to_all | solution.py:100
  283.3 16.5 %copy.96 = f32[2,4,2048,256]{3,2,1,0:T(8,128)} copy(f32[2,4,2048,256]{2,3,1,0:T(8,128)} %bitcast.175) | data formatting | bytes 33554432 | tf_op jit(solution)/shard_map/all_to_all | solution.py:100
  299.8 26.3 %fusion.15 = f32[2,32,256,256]{3,1,2,0:T(8,128)} fusion(f32[2,32,256,256]{3,2,1,0:T(8,128)} %bitcast.174, f32[1,32,2,32]{3,1,2,0:T(8,128)S(1)} %get-tuple-element.27, f32[1,32,2,32]{3,1,2,0:T(8,128)S(1)} %get-tuple-element.26), kind=kOutput, calls=%fused_computation.27 | convolution fusion | flops 1610616832 | bytes 33570816 | tf_op jit(solution)/shard_map/aibq,bqpc->aipc/dot_general | solution.py:77
  326.1 13.7 %multiply_subtract_fusion.3 = (f32[1,32,256,256]{3,1,2,0:T(8,128)}, f32[1,32,256,256]{3,1,2,0:T(8,128)}) fusion(f32[2,32,256,256]{3,1,2,0:T(8,128)} %fusion.15, f32[32,256]{0,1:T(8,128)S(1)} %copy-done.3, f32[32,256]{0,1:T(8,128)S(1)} %get-tuple-element.42), kind=kLoop, calls=%fused_computation.26 | loop fusion | flops 12582912 | bytes 33619968 | tf_op jit(solution)/shard_map/sub | solution.py:23
  339.8 6.6 pad_maximum_fusion
  346.4 42.2 %convolution_bitcast_fusion.1 = f32[2,512,32,256]{3,1,2,0:T(8,128)} fusion(f32[2,32,256,256]{3,1,2,0:T(8,128)S(1)} %pad_maximum_fusion, f32[1,512,2,256]{3,1,2,0:T(8,128)S(1)} %get-tuple-element.19, f32[1,512,2,256]{3,1,2,0:T(8,128)S(1)} %get-tuple-element.18), kind=kOutput, calls=%fused_computation.7 | convolution fusion | flops 25770328064 | bytes 52428800 | tf_op jit(solution)/shard_map/agbp,bipc->agic/dot_general | solution.py:77
  388.6 22.0 %multiply_subtract_fusion.1 = (f32[1,512,32,256]{3,1,2,0:T(8,128)}, f32[1,512,32,256]{3,1,2,0:T(8,128)}) fusion(f32[2,512,32,256]{3,1,2,0:T(8,128)} %convolution_bitcast_fusion.1, f32[512,256]{1,0:T(8,128)S(1)} %get-tuple-element.29, f32[512,256]{1,0:T(8,128)S(1)} %get-tuple-element.30), kind=kLoop, calls=%fused_computation.21 | loop fusion | flops 25165824 | bytes 68157440 | tf_op jit(solution)/shard_map/sub | solution.py:23
  410.6 22.8 %fusion.22 = f32[512,2,32,32]{0,3,1,2:T(8,128)} fusion(f32[1,32,2,256]{3,1,2,0:T(8,128)S(1)} %get-tuple-element.21, f32[1,32,2,256]{3,1,2,0:T(8,128)S(1)} %get-tuple-element.20, f32[1,512,32,256]{3,1,2,0:T(8,128)} %get-tuple-element.11, f32[1,512,32,256]{3,1,2,0:T(8,128)} %get-tuple-element.10), kind=kOutput, calls=%fused_computation.31 | convolution fusion | flops 3230695424 | bytes 37879808 | tf_op jit(solution)/shard_map/ajbc,bgic->gaij/dot_general | solution.py:77
  433.4 5.0 copy.100
  438.5 5.4 copy.167
  444.3 143.5 %reduce-scatter.4.cloned.1.call-done = f32[16,2048]{1,0:T(8,128)} async-done(((f32[512,2048]{1,0:T(8,128)}), f32[16,2048]{1,0:T(8,128)}) %reduce-scatter.4.cloned.1.call-update) | async-done | bytes 131088
  587.8 2.2 copy.168
  590.1 2.3 fusion.282
  592.3 1.4 copy.170
  593.7 1.4 copy.169
  595.1 0.4 fusion.87
  595.5 0.4 fusion.91
  596.0 0.4 fusion.38
  596.4 0.6 fusion.168
  597.0 0.6 fusion.154
  597.6 0.4 fusion.37
  598.1 0.6 fusion.36
  598.7 0.6 fusion.35
  599.3 2.3 fusion.51
  601.6 2.3 fusion.49
  603.8 2.3 convolution_subtract_fusion.3
  606.1 3.8 fusion.80
  609.9 0.7 compare_select_fusion.1
  610.6 3.1 fusion.48
  613.7 3.1 fusion.70
  616.9 3.1 convolution_subtract_fusion.2
  620.0 3.1 convolution_add_fusion.2
  623.1 1.6 fusion.160
  624.7 1.8 fusion.164
  626.5 1.6 fusion.34
  628.2 0.6 fusion.162
  628.8 0.6 fusion.149
  629.4 1.6 fusion.33
  631.0 0.6 fusion.32
  631.6 0.6 fusion.30
  632.3 0.9 reshape.563
  633.2 1.1 fusion.135
  634.4 57.8 %all-gather.2.cloned.1.call-done = f32[512,2048]{1,0:T(8,128)} async-done(((f32[16,2048]{1,0:T(8,128)}), f32[512,2048]{1,0:T(8,128)}) %all-gather.2.cloned.1.call-update) | async-done | bytes 4194320 | tf_op jit(solution)/shard_map/all_gather | solution.py:123
  692.2 5.3 copy.117
  697.5 20.8 %convolution_bitcast_fusion = f32[2,512,32,256]{3,1,2,0:T(8,128)} fusion(f32[512,2,32,32]{0,3,2,1:T(8,128)} %bitcast.179, f32[1,32,2,256]{3,1,2,0:T(8,128)} %copy-done.2, f32[1,32,2,256]{3,1,2,0:T(8,128)S(1)} %get-tuple-element.20), kind=kOutput, calls=%fused_computation.6 | convolution fusion | flops 3221258240 | bytes 37879808 | tf_op jit(solution)/shard_map/ajbc,gaij->bgic/dot_general | solution.py:77
  718.3 17.2 %multiply_subtract_fusion = (f32[1,512,32,256]{3,1,2,0:T(8,128)S(1)}, f32[1,512,32,256]{3,1,2,0:T(8,128)}) fusion(f32[2,512,32,256]{3,1,2,0:T(8,128)} %convolution_bitcast_fusion, f32[512,256]{1,0:T(8,128)} %get-tuple-element.28, f32[512,256]{1,0:T(8,128)S(1)} %get-tuple-element.30), kind=kLoop, calls=%fused_computation.19 | loop fusion | flops 25165824 | bytes 68157440 | tf_op jit(solution)/shard_map/sub | solution.py:23
  735.5 32.3 %fusion.12 = f32[32,256,2,256]{3,1,2,0:T(8,128)} fusion(f32[1,512,32,256]{3,1,2,0:T(8,128)} %get-tuple-element.9, f32[1,512,32,256]{3,1,2,0:T(8,128)S(1)} %get-tuple-element.8, f32[1,512,2,256]{3,1,2,0:T(8,128)S(1)} %get-tuple-element.19, f32[1,512,2,256]{3,1,2,0:T(8,128)S(1)} %get-tuple-element.18), kind=kOutput, calls=%fused_computation.22 | convolution fusion | flops 25778716672 | bytes 52428800 | tf_op jit(solution)/shard_map/agbp,agic->bipc/dot_general | solution.py:77
  767.8 20.2 %copy.123 = f32[32,256,2,256]{1,0,3,2:T(8,128)} copy(f32[32,256,2,256]{3,1,2,0:T(8,128)} %fusion.12) | data formatting | bytes 33554432 | tf_op jit(solution)/shard_map/agbp,agic->bipc/dot_general | solution.py:77
  788.1 9.8 multiply_subtract_fusion.2
  797.9 13.8 %fusion.18 = f32[2,32,256,256]{3,1,2,0:T(8,128)} fusion(f32[1,32,256,256]{3,1,2,0:T(8,128)} %get-tuple-element.13, f32[1,32,256,256]{3,1,2,0:T(8,128)S(1)} %get-tuple-element.12, f32[1,32,2,32]{3,1,2,0:T(8,128)S(1)} %copy-done.8, f32[1,32,2,32]{3,1,2,0:T(8,128)S(1)} %copy-done.6), kind=kOutput, calls=%fused_computation.28 | convolution fusion | flops 1619005440 | bytes 33570816 | tf_op jit(solution)/shard_map/aibq,aipc->bqpc/dot_general | solution.py:77
  811.7 15.5 %copy.126 = f32[2,32,256,256]{3,2,1,0:T(8,128)S(1)} copy(f32[2,32,256,256]{3,1,2,0:T(8,128)} %fusion.18) | data formatting | bytes 33554432 | tf_op jit(solution)/shard_map/aibq,aipc->bqpc/dot_general | solution.py:77
  827.2 46.1 %copy.127 = f32[2,8192,256]{2,0,1:T(2,128)} copy(f32[2,8192,256]{2,1,0:T(8,128)S(1)} %bitcast.176) | data formatting | bytes 33554432 | tf_op jit(solution)/shard_map/reshape | solution.py:131
  873.3 7.0 all-to-all-start.1
  880.3 0.6 pad_maximum_fusion.5
  880.9 182.4 %all-to-all-done.1 = f32[2,8192,256]{2,0,1:T(2,128)} async-done(((f32[2,8192,256]{2,0,1:T(2,128)}), f32[2,8192,256]{2,0,1:T(2,128)}, u32[]{:S(2)}, u32[]{:S(2)}) %all-to-all-start.1) | async-done | bytes 16777248 | tf_op jit(solution)/shard_map/all_to_all | solution.py:130
  1063.3 12.8 %copy.128 = f32[2,8192,256]{2,1,0:T(8,128)} copy(f32[2,8192,256]{2,0,1:T(2,128)} %all-to-all-done.1) | data formatting | bytes 33554432 | tf_op jit(solution)/shard_map/all_to_all | solution.py:130
  1076.2 16.4 %copy.129 = f32[2,2048,4,256]{1,3,2,0:T(8,128)} copy(f32[2,2048,4,256]{3,1,2,0:T(8,128)} %bitcast.177) | data formatting | bytes 33554432 | tf_op jit(solution)/shard_map/all_to_all | solution.py:130
  1092.6 18.0 %copy.130 = f32[2,2048,1024]{2,1,0:T(8,128)} copy(f32[2,2048,1024]{1,2,0:T(8,128)} %bitcast.178) | data formatting | bytes 33554432
  (53 shorter events, 1.2 us)
Async XLA Ops:
  32.4 7.2 copy-start.12
  32.4 7.2 copy-start.13
  32.5 233.1 %all-to-all-start = ((f32[2,2048,1024]{1,0,2:T(2,128)}), f32[2,2048,1024]{1,0,2:T(2,128)}, u32[]{:S(2)}, u32[]{:S(2)}) async-start(f32[2,2048,1024]{1,0,2:T(2,128)} %copy.94), calls=%async_computation | async-start | bytes 33554432 | tf_op jit(solution)/shard_map/all_to_all | solution.py:100
  39.6 548.3 %reduce-scatter.4.cloned.1.call-start = ((), (), s32[]{:S(2)}) async-start(), calls=%async_computation.4 | async-start | bytes 4325376
  258.6 41.1 %copy-start.5 = (f32[1,32,2,32]{3,1,2,0:T(8,128)}, f32[1,32,2,32]{3,1,2,0:T(8,128)S(1)}, u32[]{:S(2)}) copy-start(f32[1,32,2,32]{3,1,2,0:T(8,128)S(1)} %get-tuple-element.26) | copy-start | bytes 24580
  258.7 41.1 %copy-start.7 = (f32[1,32,2,32]{3,1,2,0:T(8,128)}, f32[1,32,2,32]{3,1,2,0:T(8,128)S(1)}, u32[]{:S(2)}) copy-start(f32[1,32,2,32]{3,1,2,0:T(8,128)S(1)} %get-tuple-element.27) | copy-start | bytes 24580
  258.8 151.8 %copy-start.2 = (f32[1,32,2,256]{3,1,2,0:T(8,128)}, f32[1,32,2,256]{3,1,2,0:T(8,128)S(1)}, u32[]{:S(2)}) copy-start(f32[1,32,2,256]{3,1,2,0:T(8,128)S(1)} %get-tuple-element.21) | copy-start | bytes 196612
  260.0 66.0 %copy-start = (f32[32,256]{0,1:T(8,128)}, f32[32,256]{0,1:T(8,128)S(1)}, u32[]{:S(2)}) copy-start(f32[32,256]{0,1:T(8,128)S(1)} %get-tuple-element.42) | copy-start | bytes 98308
  299.8 26.3 %copy-start.3 = (f32[32,256]{0,1:T(8,128)S(1)}, f32[32,256]{0,1:T(8,128)}, u32[]{:S(2)}) copy-start(f32[32,256]{0,1:T(8,128)} %get-tuple-element.41) | copy-start | bytes 98308
  433.4 10.8 copy-start.14
  433.4 10.9 copy-start.10
  433.4 176.4 %copy-start.9 = (f32[16,2,128]{2,1,0:T(2,128)S(1)}, f32[16,2,128]{2,1,0:T(2,128)}, u32[]{:S(2)}) copy-start(f32[16,2,128]{2,1,0:T(2,128)} %param.9) | copy-start | bytes 49156
  443.9 248.3 %all-gather.2.cloned.1.call-start = ((), (), s32[]{:S(2)}) async-start(), calls=%async_computation.3 | async-start | bytes 4325376 | tf_op jit(solution)/shard_map/all_gather | solution.py:123
  444.2 165.7 %copy-start.11 = (f32[32]{0:T(128)}, f32[32]{0:T(128)S(1)}, u32[]{:S(2)}) copy-start(f32[32]{0:T(128)S(1)} %fusion.207) | copy-start | bytes 388
  767.8 20.2 %copy-start.1 = (f32[32,256]{0,1:T(8,128)S(1)}, f32[32,256]{0,1:T(8,128)}, u32[]{:S(2)}) copy-start(f32[32,256]{0,1:T(8,128)} %copy-done) | copy-start | bytes 98308
  767.8 20.2 %copy-start.4 = (f32[32,256]{0,1:T(8,128)S(1)}, f32[32,256]{0,1:T(8,128)}, u32[]{:S(2)}) copy-start(f32[32,256]{0,1:T(8,128)} %fusion.135) | copy-start | bytes 98308
  788.1 9.8 copy-start.6
  788.1 9.8 copy-start.8
  873.3 190.0 %all-to-all-start.1 = ((f32[2,8192,256]{2,0,1:T(2,128)}), f32[2,8192,256]{2,0,1:T(2,128)}, u32[]{:S(2)}, u32[]{:S(2)}) async-start(f32[2,8192,256]{2,0,1:T(2,128)} %copy.127), calls=%async_computation.1 | async-start | bytes 33554432 | tf_op jit(solution)/shard_map/all_to_all | solution.py:130
Sparse Core Ops, SparseCore 0:
  444.0 143.7 reduce-scatter.3
  633.3 58.8 all-gather.1
